TPU v7x, 256 devices: a whole 4x4x8 slice. The times are simulated.
256 devices in a mesh: neur: 32 (over y, z_hi, core), tm: 8 (over x, z_lo).
Axes of the slice: x: 4, y: 4, z: 8 (z_hi: 4, z_lo: 2; z = z_hi * 2 + z_lo), core: 2. Of those that a mesh axis runs over, the one named last changes fastest.
Arguments:
- spikes: int32 [1024, 262144], P(None, ('neur', 'tm')), may hold values from 0 to 9
- held_in: int32 [262144], P(('neur', 'tm')), may hold values 0 or 1
- readin_weight: bfloat16 [262144, 1024], P(('neur', 'tm')), may hold values from -0.01171875 to 0.01171875
- qkv_weight: bfloat16 [1024, 3, 1024], P(None, None, 'tm'), may hold values from -0.1875 to 0.1875
- out_weight: bfloat16 [1024, 1024], P('tm'), may hold values from -0.1875 to 0.1875
- up_weight: bfloat16 [1024, 4096], P(None, 'tm'), may hold values from -0.1875 to 0.1875
- down_weight: bfloat16 [4096, 1024], P('tm'), may hold values from -0.09375 to 0.09375
- norm_gain: float32 [1024], replicated, may hold values from 0.25 to 1.75
- mlp_gain: float32 [1024], replicated, may hold values from 0.25 to 1.75
- final_gain: float32 [1024], replicated, may hold values from 0.25 to 1.75
- readout_weight: bfloat16 [262144, 1024], P(('neur', 'tm')), may hold values from -0.1875 to 0.1875
- readout_bias: float32 [262144], P(('neur', 'tm')), may hold values from -3 to 3
Outputs:
- latents: bfloat16 [1024, 1024], P('neur')
- neuron_bits: float32 [262144], P(('neur', 'tm'))
- bits_per_spike: float32 [], replicated
All inputs are finite; a program needn't handle non-finite values. No bound on the sum of `held_in` on one device may be relied on, other than what follows from the above.
Results may differ from a plain program's by a relative error of at most 0.006.
Values may be sent and summed in bfloat16 or wider, within the bound.
No kernel may reach another device: no remote copies, remote signals or barrier semaphores. Data moves between devices by JAX's collectives and lax.ppermute only.
A program may use at most 64 MiB of HBM per device.

v0:
```python
import math
import jax
import jax.numpy as jnp
from jax import lax
from jax.sharding import PartitionSpec as P

HEAD_DIM = 128


def normed(values, gain_vec):
    return values * lax.rsqrt(jnp.mean(values * values, -1, keepdims=True) + 1e-05) * gain_vec


def on_device(
    spikes,
    held_in,
    readin_weight,
    qkv_weight,
    out_weight,
    up_weight,
    down_weight,
    norm_gain,
    mlp_gain,
    final_gain,
    readout_weight,
    readout_bias,
):
    frames_all = spikes.shape[0]
    rows_here = frames_all // lax.axis_size("neur")
    masked = (spikes * held_in[None, :]).astype(jnp.bfloat16)
    heldout = (1 - held_in).astype(jnp.float32)
    counts = jnp.sum(spikes, 0).astype(jnp.float32)
    partial_sum = jnp.dot(masked, readin_weight, preferred_element_type=jnp.float32)
    summed = lax.psum(partial_sum, ("neur", "tm"))
    stream = lax.dynamic_slice_in_dim(summed, lax.axis_index("neur") * rows_here, rows_here, 0)
    model_dim = stream.shape[1]
    head_cols = qkv_weight.shape[2]
    local_heads = head_cols // HEAD_DIM
    attn_in = normed(stream, norm_gain).astype(jnp.bfloat16)
    projected = jnp.dot(
        attn_in, qkv_weight.reshape(model_dim, 3 * head_cols), preferred_element_type=jnp.float32
    ).astype(jnp.bfloat16)
    queries = projected[:, :head_cols].reshape(rows_here, local_heads, HEAD_DIM)
    keys_local = projected[:, head_cols : 2 * head_cols]
    values_local = projected[:, 2 * head_cols :]
    scaling = 1.0 / math.sqrt(HEAD_DIM)
    key_rows = lax.all_gather(keys_local, "neur", axis=0, tiled=True).reshape(
        -1, local_heads, HEAD_DIM
    )
    value_rows = lax.all_gather(values_local, "neur", axis=0, tiled=True).reshape(
        -1, local_heads, HEAD_DIM
    )
    scores = (
        jnp.einsum("qhd,khd->hqk", queries, key_rows, preferred_element_type=jnp.float32) * scaling
    )
    weights = jnp.exp(scores)
    numerator = jnp.einsum(
        "hqk,khd->qhd", weights.astype(jnp.bfloat16), value_rows, preferred_element_type=jnp.float32
    )
    denominator = jnp.sum(weights, -1).T
    numerator, denominator = (numerator, denominator)
    heads_out = (
        (numerator / denominator[:, :, None]).astype(jnp.bfloat16).reshape(rows_here, head_cols)
    )
    attn_part = jnp.dot(heads_out, out_weight, preferred_element_type=jnp.float32)
    mixed_state = stream + lax.psum(attn_part, "tm")
    mlp_in = normed(mixed_state, mlp_gain).astype(jnp.bfloat16)
    hidden_act = jax.nn.gelu(jnp.dot(mlp_in, up_weight, preferred_element_type=jnp.float32)).astype(
        jnp.bfloat16
    )
    mlp_part = jnp.dot(hidden_act, down_weight, preferred_element_type=jnp.float32)
    final_state = mixed_state + lax.psum(mlp_part, "tm")
    latents = normed(final_state, final_gain).astype(jnp.bfloat16)
    log_rate = (
        lax.dot_general(
            lax.all_gather(latents, "neur", axis=0, tiled=True),
            readout_weight,
            (((1,), (1,)), ((), ())),
            preferred_element_type=jnp.float32,
        )
        + readout_bias[None, :]
    )
    observed = spikes.astype(jnp.float32)
    model_ll = jnp.sum(observed * log_rate - jnp.exp(log_rate), 0)
    null_ll = counts * jnp.log((counts + 1.0) / frames_all) - (counts + 1.0)
    gained = heldout * (model_ll - null_ll)
    neuron_bits = gained / (math.log(2.0) * (counts + 1.0))
    score_sum, spike_sum = lax.psum((jnp.sum(gained), jnp.sum(heldout * counts)), ("neur", "tm"))
    bits_total = score_sum / (math.log(2.0) * (1.0 + spike_sum))
    return (latents, neuron_bits, bits_total)


def solution(mesh):
    in_specs = (
        P(None, ("neur", "tm")),
        P(("neur", "tm")),
        P(("neur", "tm"), None),
        P(None, None, "tm"),
        P("tm", None),
        P(None, "tm"),
        P("tm", None),
        P(),
        P(),
        P(),
        P(("neur", "tm"), None),
        P(("neur", "tm")),
    )
    out_specs = (P("neur", None), P(("neur", "tm")), P())
    return jax.shard_map(
        on_device, mesh=mesh, in_specs=in_specs, out_specs=out_specs, check_vma=False
    )
```

profile of v0, /device:TPU:1, one launch (start us, length us, event | category | flops | bytes accessed | tf_op | source)
XLA Modules:
  0.0 675.9 jit_solution(17022954513759164385)
XLA Ops:
  7.2 0.0 copy-start
  7.2 0.0 all-reduce.5.cloned.1.call-start
  7.2 1.5 copy-done
  8.8 6.5 fusion
  15.3 0.0 copy-start.2
  15.3 0.0 copy-start.1
  15.3 0.0 copy-start.5
  15.3 0.0 all-reduce.5.cloned.1.call-update
  15.3 0.0 copy-start.3
  15.3 0.0 all-reduce.7.cloned.1.call-start
  15.4 1.4 copy.15
  16.8 269.4 %all-reduce.5.cloned.1.call-done = f32[1024,1024]{1,0:T(8,128)} async-done(((f32[1024,1024]{1,0:T(8,128)}), f32[1024,1024]{1,0:T(8,128)}) %all-reduce.5.cloned.1.call-update) | async-done | bytes 4194320 | tf_op jit(solution)/shard_map/psum | solution.py:34
  286.2 1.0 multiply_reduce_fusion.2
  287.2 0.0 copy-done.2
  287.2 1.2 convolution_convert_fusion
  288.5 42.8 %all_gather.10 = bf16[1024,128]{1,0:T(8,128)(2,1)S(1)} all-gather(bf16[32,128]{1,0:T(8,128)(2,1)S(1)} %get-tuple-element.11), channel_id=1, replica_groups=mesh['neur'=32,'tm'=8] {'neur'}, dimensions={0}, use_global_device_ids=true | all-gather | bytes 270336 | tf_op jit(solution)/shard_map/all_gather | solution.py:47
  331.3 0.3 fusion.38
  331.6 42.1 %all_gather.9 = bf16[1024,128]{1,0:T(8,128)(2,1)S(1)} all-gather(bf16[32,128]{1,0:T(8,128)(2,1)S(1)} %get-tuple-element.12), channel_id=1, replica_groups=mesh['neur'=32,'tm'=8] {'neur'}, dimensions={0}, use_global_device_ids=true | all-gather | bytes 270336 | tf_op jit(solution)/shard_map/all_gather | solution.py:50
  373.7 0.0 copy-done.1
  373.7 0.0 copy-start.6
  373.7 0.9 fusion.6
  374.6 0.0 all-reduce.7.cloned.1.call-update
  374.6 0.0 all-reduce.9.cloned.1.call-start
  374.7 67.4 %all-reduce.7.cloned.1.call-done = f32[32,1024]{1,0:T(8,128)} async-done(((f32[32,1024]{1,0:T(8,128)}), f32[32,1024]{1,0:T(8,128)}) %all-reduce.7.cloned.1.call-update) | async-done | bytes 131088 | tf_op jit(solution)/shard_map/psum | solution.py:66
  442.1 1.1 multiply_reduce_fusion.1
  443.2 0.0 copy-done.5
  443.2 2.8 fusion.16
  446.0 0.0 all-reduce.9.cloned.1.call-update
  446.0 0.0 all-gather.2.cloned.1.call-start
  446.1 76.6 %all-reduce.9.cloned.1.call-done = f32[32,1024]{1,0:T(8,128)} async-done(((f32[32,1024]{1,0:T(8,128)}), f32[32,1024]{1,0:T(8,128)}) %all-reduce.9.cloned.1.call-update) | async-done | bytes 131088 | tf_op jit(solution)/shard_map/psum | solution.py:72
  522.6 1.0 multiply_reduce_fusion
  523.7 0.0 copy-done.3
  523.7 0.7 multiply_convert_fusion.2
  524.4 0.0 all-gather.2.cloned.1.call-update
  524.4 2.5 reduce_sum.77
  526.9 0.0 copy-start.4
  526.9 58.2 %all-gather.2.cloned.1.call-done = bf16[1024,1024]{1,0:T(8,128)(2,1)} async-done(((bf16[32,1024]{1,0:T(8,128)(2,1)}), bf16[1024,1024]{1,0:T(8,128)(2,1)}) %all-gather.2.cloned.1.call-update) | async-done | bytes 2097168 | tf_op jit(solution)/shard_map/all_gather | solution.py:76
  585.1 0.0 copy-done.6
  585.1 6.2 subtract_reduce_fusion
  591.3 0.0 copy-done.4
  591.3 1.3 multiply_reduce_fusion.3
  592.6 74.4 %all-reduce = (f32[]{:T(128)}, f32[]{:T(128)}) all-reduce(f32[]{:T(128)} %get-tuple-element.4, f32[]{:T(128)} %get-tuple-element.3), channel_id=1, replica_groups=mesh['neur'=32,'tm'=8] {'neur','tm'}, use_global_device_ids=true, to_apply=%region_10.0 | all-reduce | flops 2 | bytes 16 | tf_op jit(solution)/shard_map/psum | solution.py:88
  (4 shorter events, 0.0 us)
Async XLA Ops:
  7.2 1.6 copy-start
  7.2 279.0 %all-reduce.5.cloned.1.call-start = ((), (), s32[]{:S(2)}) async-start(), calls=%async_computation | async-start | bytes 8388608 | tf_op jit(solution)/shard_map/psum | solution.py:34
  15.3 271.9 %copy-start.2 = (f32[1024]{0:T(1024)S(1)}, f32[1024]{0:T(1024)}, u32[]{:S(2)}) copy-start(f32[1024]{0:T(1024)} %param.19) | copy-start | bytes 12292
  15.3 358.4 %copy-start.1 = (bf16[128,1024]{1,0:T(8,128)(2,1)S(1)}, bf16[128,1024]{1,0:T(8,128)(2,1)}, u32[]{:S(2)}) copy-start(bf16[128,1024]{1,0:T(8,128)(2,1)} %param.16) | copy-start | bytes 786436
  15.3 428.0 %copy-start.5 = (f32[1024]{0:T(1024)S(1)}, f32[1024]{0:T(1024)}, u32[]{:S(2)}) copy-start(f32[1024]{0:T(1024)} %param.20) | copy-start | bytes 12292
  15.3 508.4 %copy-start.3 = (f32[1024]{0:T(1024)S(1)}, f32[1024]{0:T(1024)}, u32[]{:S(2)}) copy-start(f32[1024]{0:T(1024)} %param.21) | copy-start | bytes 12292
  15.3 426.8 %all-reduce.7.cloned.1.call-start = ((), (), s32[]{:S(2)}) async-start(), calls=%async_computation.1 | async-start | bytes 262144 | tf_op jit(solution)/shard_map/psum | solution.py:66
  373.7 211.5 %copy-start.6 = (f32[1024]{0:T(1024)S(1)}, f32[1024]{0:T(1024)}, u32[]{:S(2)}) copy-start(f32[1024]{0:T(1024)} %param.23) | copy-start | bytes 12292
  374.6 148.0 %all-reduce.9.cloned.1.call-start = ((), (), s32[]{:S(2)}) async-start(), calls=%async_computation.2 | async-start | bytes 262144 | tf_op jit(solution)/shard_map/psum | solution.py:72
  446.0 139.1 %all-gather.2.cloned.1.call-start = ((), (), s32[]{:S(2)}) async-start(), calls=%async_computation.3 | async-start | bytes 2162688 | tf_op jit(solution)/shard_map/all_gather | solution.py:76
  526.9 64.4 %copy-start.4 = (s32[1024]{0:T(1024)S(1)}, s32[1024]{0:T(1024)}, u32[]{:S(2)}) copy-start(s32[1024]{0:T(1024)} %param.13) | copy-start | bytes 12292
Sparse Core Ops, SparseCore 0:
  15.4 270.7 all-reduce.4
  374.8 67.3 all-reduce.6
  446.2 76.4 all-reduce.8
  526.0 59.1 all-gather.1
where the time goes:
time: 676 us
  waiting for transfers between devices  472 us (70%)
  blocking collectives  159 us (24%)
  matrix products  18 us (3%)
  between operations  16.2 us (2%)
  other arithmetic  7.64 us (1%)
    psum x1, waiting for transfers between devices, on_device(): summed = lax.psum(partial_sum, ('neur', 'tm'))  269 us
    psum x1, waiting for transfers between devices, on_device(): final_state = mixed_state + lax.psum(mlp_part, 'tm')  76.6 us
    psum x1, blocking collectives, on_device(): lax.psum((jnp.sum(gained), jnp.sum(heldout * counts)), ('neur', 'tm'))  74.4 us
    psum x1, waiting for transfers between devices, on_device(): mixed_state = stream + lax.psum(attn_part, 'tm')  67.4 us
    all_gather x1, waiting for transfers between devices, on_device(): lax.all_gather(latents, 'neur', axis=0, tiled=True)  58.2 us
    all_gather x1, blocking collectives, on_device(): lax.all_gather(keys_local, 'neur', axis=0, tiled=True)  42.8 us
    all_gather x1, blocking collectives, on_device(): lax.all_gather(values_local, 'neur', axis=0, tiled=True)  42.1 us
  transfers between devices with their start and end apart: 4, of which 4 were waited for; matrix products, arithmetic and copies ran while one was open for 1% of the time, Pallas kernels for 0%

commit v1 on v0

--- a/solution.py
+++ b/solution.py
@@ -5,6 +5,11 @@
 from jax.sharding import PartitionSpec as P
 
 HEAD_DIM = 128
+
+
+def exchange_gather(shard, axis, along):
+    sent = jnp.stack([shard] * lax.axis_size(axis))
+    return jnp.concatenate(lax.all_to_all(sent, axis, 0, 0), axis=along)
 
 
 def normed(values, gain_vec):
@@ -47,9 +52,7 @@
     key_rows = lax.all_gather(keys_local, "neur", axis=0, tiled=True).reshape(
         -1, local_heads, HEAD_DIM
     )
-    value_rows = lax.all_gather(values_local, "neur", axis=0, tiled=True).reshape(
-        -1, local_heads, HEAD_DIM
-    )
+    value_rows = exchange_gather(values_local, "neur", 0).reshape(-1, local_heads, HEAD_DIM)
     scores = (
         jnp.einsum("qhd,khd->hqk", queries, key_rows, preferred_element_type=jnp.float32) * scaling
     )

time: 676 us -> 646 us (0.956)
  blocking collectives: 159 us -> 120 us
  starting transfers between devices: 0.16 us -> 10.6 us
    all_gather x1 -> x0, blocking collectives: 42.1 us -> none  [on_device(): lax.all_gather(values_local, 'neur', axis=0, tiled=True)]
    all_to_all x0 -> x1, starting transfers between devices: none -> 10.4 us  [exchange_gather(): return jnp.concatenate(lax.all_to_all(sent, axis, 0, 0), axis=along)]
  transfers between devices with their start and end apart: 4 -> 5, of which waited for: 4 -> 4; matrix products, arithmetic and copies ran while one was open for 1% -> 1% of each run, Pallas kernels for 0% -> 0%
where the time goes in v1:
time: 646 us
  waiting for transfers between devices  470 us (73%)
  blocking collectives  120 us (19%)
  matrix products  18 us (3%)
  between operations  16.2 us (3%)
  starting transfers between devices  10.6 us (2%)
  other arithmetic  7.64 us (1%)
    psum x1, waiting for transfers between devices, on_device(): summed = lax.psum(partial_sum, ('neur', 'tm'))  269 us
    psum x1, waiting for transfers between devices, on_device(): final_state = mixed_state + lax.psum(mlp_part, 'tm')  76.6 us
    psum x1, blocking collectives, on_device(): lax.psum((jnp.sum(gained), jnp.sum(heldout * counts)), ('neur', 'tm'))  74.4 us
    psum x1, waiting for transfers between devices, on_device(): mixed_state = stream + lax.psum(attn_part, 'tm')  65.4 us
    all_gather x1, waiting for transfers between devices, on_device(): lax.all_gather(latents, 'neur', axis=0, tiled=True)  58.2 us
    all_gather x1, blocking collectives, on_device(): lax.all_gather(keys_local, 'neur', axis=0, tiled=True)  45.7 us
  transfers between devices with their start and end apart: 5, of which 4 were waited for; matrix products, arithmetic and copies ran while one was open for 1% of the time, Pallas kernels for 0%

profile of v1, /device:TPU:1, one launch (start us, length us, event | category | flops | bytes accessed | tf_op | source)
XLA Modules:
  0.0 645.9 jit_solution(1866164208887646817)
XLA Ops:
  7.2 0.0 copy-start
  7.2 0.0 all-reduce.5.cloned.1.call-start
  7.2 1.5 copy-done
  8.8 6.5 %fusion = f32[1024,1024]{1,0:T(8,128)} fusion(bf16[1024,1024]{1,0:T(8,128)(2,1)S(1)} %copy-done, s32[1024,1024]{1,0:T(8,128)} %param.12, s32[1024]{0:T(1024)} %param.13), kind=kOutput, calls=%fused_computation.2 | convolution fusion | flops 2149580800 | bytes 10489856 | tf_op jit(solution)/shard_map/dot_general | solution.py:38
  15.3 0.0 copy-start.2
  15.3 0.0 copy-start.1
  15.3 0.0 copy-start.5
  15.3 0.0 all-reduce.5.cloned.1.call-update
  15.3 0.0 copy-start.3
  15.3 1.4 copy.15
  16.8 269.4 %all-reduce.5.cloned.1.call-done = f32[1024,1024]{1,0:T(8,128)} async-done(((f32[1024,1024]{1,0:T(8,128)}), f32[1024,1024]{1,0:T(8,128)}) %all-reduce.5.cloned.1.call-update) | async-done | bytes 4194320 | tf_op jit(solution)/shard_map/psum | solution.py:39
  286.2 1.0 multiply_reduce_fusion.2
  287.2 0.0 copy-done.2
  287.2 1.2 convolution_convert_fusion
  288.5 0.7 stack.2
  289.2 10.4 %all-to-all-start = ((bf16[32,32,128]{2,1,0:T(8,128)(2,1)}), bf16[32,32,128]{2,1,0:T(8,128)(2,1)S(1)}, u32[]{:S(2)}, u32[]{:S(2)}) async-start(bf16[32,32,128]{2,1,0:T(8,128)(2,1)} %stack.2), calls=%async_computation | async-start | bytes 524288 | tf_op jit(solution)/shard_map/all_to_all | solution.py:12
  299.6 0.0 all-reduce.7.cloned.1.call-start
  299.7 45.7 %all_gather.6 = bf16[1024,128]{1,0:T(8,128)(2,1)S(1)} all-gather(bf16[32,128]{1,0:T(8,128)(2,1)S(1)} %get-tuple-element.11), channel_id=1, replica_groups=mesh['neur'=32,'tm'=8] {'neur'}, dimensions={0}, use_global_device_ids=true | all-gather | bytes 270336 | tf_op jit(solution)/shard_map/all_gather | solution.py:52
  345.4 0.3 fusion.38
  345.7 0.0 all-to-all-done
  345.7 0.0 copy-done.1
  345.7 0.0 copy-start.6
  345.7 1.0 fusion.6
  346.6 0.0 all-reduce.7.cloned.1.call-update
  346.7 0.0 all-reduce.9.cloned.1.call-start
  346.7 65.4 %all-reduce.7.cloned.1.call-done = f32[32,1024]{1,0:T(8,128)} async-done(((f32[32,1024]{1,0:T(8,128)}), f32[32,1024]{1,0:T(8,128)}) %all-reduce.7.cloned.1.call-update) | async-done | bytes 131088 | tf_op jit(solution)/shard_map/psum | solution.py:69
  412.1 1.1 multiply_reduce_fusion.1
  413.2 0.0 copy-done.5
  413.2 2.8 fusion.16
  416.0 0.0 all-reduce.9.cloned.1.call-update
  416.1 0.0 all-gather.2.cloned.1.call-start
  416.1 76.6 %all-reduce.9.cloned.1.call-done = f32[32,1024]{1,0:T(8,128)} async-done(((f32[32,1024]{1,0:T(8,128)}), f32[32,1024]{1,0:T(8,128)}) %all-reduce.9.cloned.1.call-update) | async-done | bytes 131088 | tf_op jit(solution)/shard_map/psum | solution.py:75
  492.7 1.0 multiply_reduce_fusion
  493.7 0.0 copy-done.3
  493.7 0.7 multiply_convert_fusion.2
  494.4 0.0 all-gather.2.cloned.1.call-update
  494.5 2.5 reduce_sum.77
  496.9 0.0 copy-start.4
  496.9 58.2 %all-gather.2.cloned.1.call-done = bf16[1024,1024]{1,0:T(8,128)(2,1)} async-done(((bf16[32,1024]{1,0:T(8,128)(2,1)}), bf16[1024,1024]{1,0:T(8,128)(2,1)}) %all-gather.2.cloned.1.call-update) | async-done | bytes 2097168 | tf_op jit(solution)/shard_map/all_gather | solution.py:79
  555.2 0.0 copy-done.6
  555.2 6.2 subtract_reduce_fusion
  561.4 0.0 copy-done.4
  561.4 1.3 multiply_reduce_fusion.3
  562.7 74.4 %all-reduce = (f32[]{:T(128)}, f32[]{:T(128)}) all-reduce(f32[]{:T(128)} %get-tuple-element.4, f32[]{:T(128)} %get-tuple-element.3), channel_id=1, replica_groups=mesh['neur'=32,'tm'=8] {'neur','tm'}, use_global_device_ids=true, to_apply=%region_10.0 | all-reduce | flops 2 | bytes 16 | tf_op jit(solution)/shard_map/psum | solution.py:91
  (4 shorter events, 0.0 us)
Async XLA Ops:
  7.2 1.6 copy-start
  7.2 279.0 %all-reduce.5.cloned.1.call-start = ((), (), s32[]{:S(2)}) async-start(), calls=%async_computation.1 | async-start | bytes 8388608 | tf_op jit(solution)/shard_map/psum | solution.py:39
  15.3 271.9 %copy-start.2 = (f32[1024]{0:T(1024)S(1)}, f32[1024]{0:T(1024)}, u32[]{:S(2)}) copy-start(f32[1024]{0:T(1024)} %param.19) | copy-start | bytes 12292
  15.3 330.4 %copy-start.1 = (bf16[128,1024]{1,0:T(8,128)(2,1)S(1)}, bf16[128,1024]{1,0:T(8,128)(2,1)}, u32[]{:S(2)}) copy-start(bf16[128,1024]{1,0:T(8,128)(2,1)} %param.16) | copy-start | bytes 786436
  15.3 398.0 %copy-start.5 = (f32[1024]{0:T(1024)S(1)}, f32[1024]{0:T(1024)}, u32[]{:S(2)}) copy-start(f32[1024]{0:T(1024)} %param.20) | copy-start | bytes 12292
  15.3 478.4 %copy-start.3 = (f32[1024]{0:T(1024)S(1)}, f32[1024]{0:T(1024)}, u32[]{:S(2)}) copy-start(f32[1024]{0:T(1024)} %param.21) | copy-start | bytes 12292
  289.2 56.5 %all-to-all-start = ((bf16[32,32,128]{2,1,0:T(8,128)(2,1)}), bf16[32,32,128]{2,1,0:T(8,128)(2,1)S(1)}, u32[]{:S(2)}, u32[]{:S(2)}) async-start(bf16[32,32,128]{2,1,0:T(8,128)(2,1)} %stack.2), calls=%async_computation | async-start | bytes 524288 | tf_op jit(solution)/shard_map/all_to_all | solution.py:12
  299.6 112.5 %all-reduce.7.cloned.1.call-start = ((), (), s32[]{:S(2)}) async-start(), calls=%async_computation.2 | async-start | bytes 262144 | tf_op jit(solution)/shard_map/psum | solution.py:69
  345.7 209.5 %copy-start.6 = (f32[1024]{0:T(1024)S(1)}, f32[1024]{0:T(1024)}, u32[]{:S(2)}) copy-start(f32[1024]{0:T(1024)} %param.23) | copy-start | bytes 12292
  346.7 146.0 %all-reduce.9.cloned.1.call-start = ((), (), s32[]{:S(2)}) async-start(), calls=%async_computation.3 | async-start | bytes 262144 | tf_op jit(solution)/shard_map/psum | solution.py:75
  416.1 139.1 %all-gather.2.cloned.1.call-start = ((), (), s32[]{:S(2)}) async-start(), calls=%async_computation.4 | async-start | bytes 2162688 | tf_op jit(solution)/shard_map/all_gather | solution.py:79
  496.9 64.4 %copy-start.4 = (s32[1024]{0:T(1024)S(1)}, s32[1024]{0:T(1024)}, u32[]{:S(2)}) copy-start(s32[1024]{0:T(1024)} %param.13) | copy-start | bytes 12292
Sparse Core Ops, SparseCore 0:
  15.4 270.7 all-reduce.4
  346.8 65.3 all-reduce.6
  416.2 76.4 all-reduce.8
  496.0 59.1 all-gather.1
